TPU v7x, 128 devices: a whole 4x4x4 slice. The times are simulated.
128 devices in a mesh: wide: 16 (over y, x), narrow: 8 (over z, core).
Axes of the slice: x: 4, y: 4, z: 4, core: 2. Of those that a mesh axis runs over, the one named last changes fastest.
Arguments:
- tokens: bfloat16 [256, 128, 1536], P('wide'), may hold values from -8 to 8
- ln_gain: bfloat16 [1536], replicated, may hold values from 0.3984375 to 1.59375
- gate_weight: bfloat16 [1536, 8960], P(None, 'narrow'), may hold values from -0.15625 to 0.15625
- up_weight: bfloat16 [1536, 8960], P(None, 'narrow'), may hold values from -0.15625 to 0.15625
- down_weight: bfloat16 [8960, 1536], P('narrow'), may hold values from -0.0625 to 0.0625
- out_gain: bfloat16 [1536], replicated, may hold values from 0.25 to 1.75
- shard_ids: int32 [256], P('wide'), may hold values from 0 to 15, as said below
- slab_old: bfloat16 [262144, 1536], P(('wide', 'narrow')), may hold values from -8 to 8
- queries: bfloat16 [16, 64, 1536], P('wide'), may hold values from -12 to 12
- positives: int32 [16, 64], P('wide'), may hold values from 0 to 262399
- owners: int32 [4], replicated, may hold values from 0 to 15
Outputs:
- index_new: bfloat16 [16, 16, 2, 1536], P('wide', 'narrow')
- losses: float32 [4, 64], replicated
Inputs may be any that keep to these rules, and one draw needn't show every extreme that they name: `shard_ids`: among the 16 passages of one index of wide at most 2 have the same shard id; in every draw one shard id is held by exactly 2 passages of every index of wide.
All inputs are finite; a program needn't handle non-finite values.
Results may differ from a plain program's by a relative error of at most 0.0029.
Values may be sent and summed in bfloat16 or wider, within the bound.
No kernel may reach another device: no remote copies, remote signals or barrier semaphores. Data moves between devices by JAX's collectives and lax.ppermute only.
A program may use at most 128 MiB of HBM per device.

v0:
```python
import math
import jax
import jax.numpy as jnp
from jax import lax
from jax.sharding import PartitionSpec as P

EPS = 1e-06


def spread(x, axis, root):
    mine = lax.axis_index(axis) == root
    return lax.psum(jnp.where(mine, x, jnp.zeros_like(x)), axis)


def rms_scale(values):
    return lax.rsqrt(jnp.mean(values * values, axis=-1, keepdims=True) + EPS)


def local(
    tokens,
    ln_gain,
    gate_weight,
    up_weight,
    down_weight,
    out_gain,
    shard_ids,
    slab_old,
    queries,
    positives,
    owners,
):
    passages, seq_len, width = tokens.shape
    narrow_count = lax.axis_size("narrow")
    wide_count = lax.axis_size("wide")
    narrow_rank = lax.axis_index("narrow")
    wide_rank = lax.axis_index("wide")
    piece_width = width // narrow_count
    capacity = 2 * passages // wide_count
    values = tokens.astype(jnp.float32)
    normed = (values * rms_scale(values) * ln_gain.astype(jnp.float32)).astype(jnp.bfloat16)
    normed = normed.reshape(passages * seq_len, width)
    gate = jnp.dot(normed, gate_weight, preferred_element_type=jnp.float32)
    upward = jnp.dot(normed, up_weight, preferred_element_type=jnp.float32)
    hidden = (jax.nn.silu(gate) * upward).astype(jnp.bfloat16)
    partial_value = jnp.dot(hidden, down_weight, preferred_element_type=jnp.float32)
    pooled_part = jnp.mean(partial_value.reshape(passages, seq_len, width), axis=1)
    token_mean = jnp.mean(values, axis=1)
    offset = narrow_rank * piece_width
    pooled = lax.psum(pooled_part, "narrow") + token_mean
    norm_scale = rms_scale(pooled)
    own_piece = lax.dynamic_slice_in_dim(pooled, offset, piece_width, 1)
    gain_piece = lax.dynamic_slice_in_dim(out_gain.astype(jnp.float32), offset, piece_width, 0)
    embedding = (own_piece * norm_scale * gain_piece).astype(jnp.bfloat16)
    positions = jnp.arange(passages, dtype=jnp.int32)
    earlier = positions[:, None] > positions[None, :]
    same = shard_ids[:, None] == shard_ids[None, :]
    rank = jnp.sum((earlier & same).astype(jnp.int32), axis=1)
    slots = shard_ids * capacity + rank
    dispatch = slots[None, :] == jnp.arange(wide_count * capacity, dtype=jnp.int32)[:, None]
    outgoing = jnp.dot(dispatch.astype(jnp.bfloat16), embedding, preferred_element_type=jnp.float32)
    outgoing = outgoing.astype(jnp.bfloat16).reshape(wide_count, capacity, piece_width)
    numbers = wide_rank * passages + positions
    slot_numbers = jnp.sum(jnp.where(dispatch, numbers[None, :] + 1, 0), axis=1) - 1
    slot_numbers = slot_numbers.reshape(wide_count, capacity, 1)
    arrived, arrived_numbers = (
        lax.all_to_all(
            lax.all_to_all(outgoing, "wide", split_axis=0, concat_axis=0, tiled=True),
            "narrow",
            split_axis=0,
            concat_axis=2,
            tiled=True,
        ),
        lax.all_to_all(
            lax.all_to_all(slot_numbers, "wide", split_axis=0, concat_axis=0, tiled=True),
            "narrow",
            split_axis=0,
            concat_axis=2,
            tiled=True,
        ),
    )
    old_total = slab_old.shape[0] * wide_count * narrow_count
    new_rows = arrived.reshape(-1, width)
    new_numbers = arrived_numbers[:, :, 0].reshape(-1)
    valid = (new_numbers >= 0)[None, :]
    new_global = old_total + new_numbers
    device_linear = wide_rank * narrow_count + narrow_rank
    old_global = device_linear * slab_old.shape[0] + jnp.arange(slab_old.shape[0], dtype=jnp.int32)
    scale = 1.0 / math.sqrt(width)
    contract = (((1,), (1,)), ((), ()))
    block_size = queries.shape[1]
    step_count = owners.shape[0]

    def score_rows(block, positive):
        old_scores = (
            lax.dot_general(block, slab_old, contract, preferred_element_type=jnp.float32) * scale
        )
        new_scores = (
            lax.dot_general(block, new_rows, contract, preferred_element_type=jnp.float32) * scale
        )
        masked = jnp.where(valid, new_scores, -jnp.inf)
        local_max = jnp.maximum(jnp.max(old_scores, axis=1), jnp.max(masked, axis=1))
        hit_old = old_global[None, :] == positive[:, None]
        hit_new = valid & (new_global[None, :] == positive[:, None])
        local_positive = jnp.sum(jnp.where(hit_old, old_scores, 0.0), axis=1) + jnp.sum(
            jnp.where(hit_new, new_scores, 0.0), axis=1
        )
        largest = lax.pmax(local_max, ("wide", "narrow"))
        local_total = jnp.sum(jnp.exp(old_scores - largest[:, None]), axis=1)
        local_total = local_total + jnp.sum(
            jnp.where(valid, jnp.exp(new_scores - largest[:, None]), 0.0), axis=1
        )
        total, picked = lax.psum((local_total, local_positive), ("wide", "narrow"))
        return largest + jnp.log(total) - picked

    def step_body(step, losses):
        owner = owners[step]
        block, positive = (spread(queries[0], "wide", owner), spread(positives[0], "wide", owner))
        loss = score_rows(block, positive)
        return lax.dynamic_update_slice_in_dim(losses, loss[None, :], step, 0)

    start_losses = jnp.zeros((step_count, block_size), jnp.float32)
    losses = lax.fori_loop(0, step_count, step_body, start_losses)
    return (arrived[None], losses)


def solution(mesh):
    return jax.shard_map(
        local,
        mesh=mesh,
        in_specs=(
            P("wide", None, None),
            P(),
            P(None, "narrow"),
            P(None, "narrow"),
            P("narrow", None),
            P(),
            P("wide"),
            P(("wide", "narrow"), None),
            P("wide", None, None),
            P("wide", None),
            P(),
        ),
        out_specs=(P("wide", "narrow", None, None), P()),
        check_vma=False,
    )
```

profile of v0, /device:TPU:1, one launch (start us, length us, event | category | flops | bytes accessed | tf_op | source)
XLA Modules:
  0.0 1026.5 jit_solution(8330299875181176620)
XLA Ops:
  17.2 9.7 fusion.16
  26.9 22.3 %bitcast_reduce_fusion = f32[16,1536]{1,0:T(8,128)} fusion(bf16[1120,1536]{1,0:T(8,128)(2,1)} %param.17, bf16[2048,1536]{1,0:T(8,128)(2,1)} %bitcast.51, bf16[1536,1120]{0,1:T(8,128)(2,1)} %param.16, f32[2048,1120]{0,1:T(8,128)} %fusion.16), kind=kOutput, calls=%fused_computation.19 | convolution fusion | flops 14109745152 | bytes 22446080 | tf_op jit(solution)/shard_map/dot_general | solution.py:45
  51.8 7.6 all-to-all-start.2
  65.7 7.6 all-to-all-start.3
  78.1 32.4 %all-reduce.6.cloned.1.call-done = f32[16,1536]{1,0:T(8,128)} async-done(((f32[16,1536]{1,0:T(8,128)}), f32[16,1536]{1,0:T(8,128)}) %all-reduce.6.cloned.1.call-update) | async-done | bytes 98320 | tf_op jit(solution)/shard_map/psum | solution.py:49
  113.1 6.6 all-to-all-start
  126.2 7.2 all-to-all-start.1
  138.8 881.1 %while.14 = (s32[]{:T(128)}, f32[4,64]{1,0:T(4,128)}, s32[4]{0:T(128)}, bf16[1,64,1536]{2,1,0:T(8,128)(2,1)}, bf16[2048,1536]{1,0:T(8,128)(2,1)}, /*index=5*/pre...) while((s32[]{:T(128)}, f32[4,64]{1,0:T(4,128)}, ...), condition=%wide.region_19.20_spmd.clone, body=%wide.region_7.19_spmd.clone.sunk | while | flops 404558592 | bytes 10132520 | solution.py:122
  141.6 9.3 psum.59
  150.9 69.7 %all-reduce.8.cloned.1.call-done = bf16[64,1536]{1,0:T(8,128)(2,1)} async-done(((bf16[64,1536]{1,0:T(8,128)(2,1)}), bf16[64,1536]{1,0:T(8,128)(2,1)}) %all-reduce.8.cloned.1.call-update) | async-done | bytes 196624 | tf_op jit(solution)/shard_map/while/body/eval_jaxpr/psum | solution.py:12
  226.6 66.3 %pmax.13 = f32[64]{0:T(128)S(1)} all-reduce(f32[64]{0:T(128)S(1)} %max.11), channel_id=1, replica_groups=mesh['wide'=16,'narrow'=8] {'wide','narrow'}, use_global_device_ids=true, to_apply=%region_11.11 | all-reduce | flops 64 | bytes 512 | tf_op jit(solution)/shard_map/while/body/eval_jaxpr/pmax | solution.py:107
  294.4 62.5 %all-reduce.2 = (f32[64]{0:T(128)S(1)}, f32[64]{0:T(128)S(1)}) all-reduce(f32[64]{0:T(128)S(1)} %add.187, f32[64]{0:T(128)S(1)} %add.188), channel_id=1, replica_groups=mesh['wide'=16,'narrow'=8] {'wide','narrow'}, use_global_device_ids=true, to_apply=%region_18.18 | all-reduce | flops 128 | bytes 1024 | tf_op jit(solution)/shard_map/while/body/eval_jaxpr/psum | solution.py:112
  361.0 10.9 %psum.59 = s32[64]{0:T(128)S(1)} all-reduce(s32[64]{0:T(128)S(1)} %fusion.37), channel_id=1, replica_groups=mesh['wide'=16,'narrow'=8] {'wide'}, use_global_device_ids=true, to_apply=%region_15.15 | all-reduce | flops 64 | bytes 512 | tf_op jit(solution)/shard_map/while/body/eval_jaxpr/psum | solution.py:12
  371.8 69.6 %all-reduce.8.cloned.1.call-done = bf16[64,1536]{1,0:T(8,128)(2,1)} async-done(((bf16[64,1536]{1,0:T(8,128)(2,1)}), bf16[64,1536]{1,0:T(8,128)(2,1)}) %all-reduce.8.cloned.1.call-update) | async-done | bytes 196624 | tf_op jit(solution)/shard_map/while/body/eval_jaxpr/psum | solution.py:12
  447.4 66.4 %pmax.13 = f32[64]{0:T(128)S(1)} all-reduce(f32[64]{0:T(128)S(1)} %max.11), channel_id=1, replica_groups=mesh['wide'=16,'narrow'=8] {'wide','narrow'}, use_global_device_ids=true, to_apply=%region_11.11 | all-reduce | flops 64 | bytes 512 | tf_op jit(solution)/shard_map/while/body/eval_jaxpr/pmax | solution.py:107
  515.2 62.5 %all-reduce.2 = (f32[64]{0:T(128)S(1)}, f32[64]{0:T(128)S(1)}) all-reduce(f32[64]{0:T(128)S(1)} %add.187, f32[64]{0:T(128)S(1)} %add.188), channel_id=1, replica_groups=mesh['wide'=16,'narrow'=8] {'wide','narrow'}, use_global_device_ids=true, to_apply=%region_18.18 | all-reduce | flops 128 | bytes 1024 | tf_op jit(solution)/shard_map/while/body/eval_jaxpr/psum | solution.py:112
  583.3 9.0 psum.59
  592.3 69.5 %all-reduce.8.cloned.1.call-done = bf16[64,1536]{1,0:T(8,128)(2,1)} async-done(((bf16[64,1536]{1,0:T(8,128)(2,1)}), bf16[64,1536]{1,0:T(8,128)(2,1)}) %all-reduce.8.cloned.1.call-update) | async-done | bytes 196624 | tf_op jit(solution)/shard_map/while/body/eval_jaxpr/psum | solution.py:12
  667.9 66.3 %pmax.13 = f32[64]{0:T(128)S(1)} all-reduce(f32[64]{0:T(128)S(1)} %max.11), channel_id=1, replica_groups=mesh['wide'=16,'narrow'=8] {'wide','narrow'}, use_global_device_ids=true, to_apply=%region_11.11 | all-reduce | flops 64 | bytes 512 | tf_op jit(solution)/shard_map/while/body/eval_jaxpr/pmax | solution.py:107
  735.7 62.5 %all-reduce.2 = (f32[64]{0:T(128)S(1)}, f32[64]{0:T(128)S(1)}) all-reduce(f32[64]{0:T(128)S(1)} %add.187, f32[64]{0:T(128)S(1)} %add.188), channel_id=1, replica_groups=mesh['wide'=16,'narrow'=8] {'wide','narrow'}, use_global_device_ids=true, to_apply=%region_18.18 | all-reduce | flops 128 | bytes 1024 | tf_op jit(solution)/shard_map/while/body/eval_jaxpr/psum | solution.py:112
  802.2 11.2 %psum.59 = s32[64]{0:T(128)S(1)} all-reduce(s32[64]{0:T(128)S(1)} %fusion.37), channel_id=1, replica_groups=mesh['wide'=16,'narrow'=8] {'wide'}, use_global_device_ids=true, to_apply=%region_15.15 | all-reduce | flops 64 | bytes 512 | tf_op jit(solution)/shard_map/while/body/eval_jaxpr/psum | solution.py:12
  813.4 68.9 %all-reduce.8.cloned.1.call-done = bf16[64,1536]{1,0:T(8,128)(2,1)} async-done(((bf16[64,1536]{1,0:T(8,128)(2,1)}), bf16[64,1536]{1,0:T(8,128)(2,1)}) %all-reduce.8.cloned.1.call-update) | async-done | bytes 196624 | tf_op jit(solution)/shard_map/while/body/eval_jaxpr/psum | solution.py:12
  888.4 66.3 %pmax.13 = f32[64]{0:T(128)S(1)} all-reduce(f32[64]{0:T(128)S(1)} %max.11), channel_id=1, replica_groups=mesh['wide'=16,'narrow'=8] {'wide','narrow'}, use_global_device_ids=true, to_apply=%region_11.11 | all-reduce | flops 64 | bytes 512 | tf_op jit(solution)/shard_map/while/body/eval_jaxpr/pmax | solution.py:107
  956.2 62.5 %all-reduce.2 = (f32[64]{0:T(128)S(1)}, f32[64]{0:T(128)S(1)}) all-reduce(f32[64]{0:T(128)S(1)} %add.187, f32[64]{0:T(128)S(1)} %add.188), channel_id=1, replica_groups=mesh['wide'=16,'narrow'=8] {'wide','narrow'}, use_global_device_ids=true, to_apply=%region_18.18 | all-reduce | flops 128 | bytes 1024 | tf_op jit(solution)/shard_map/while/body/eval_jaxpr/psum | solution.py:112
  (110 shorter events, 82.9 us)
Async XLA Ops:
  7.2 10.1 copy-start
  7.2 103.3 %all-reduce.6.cloned.1.call-start = ((), (), s32[]{:S(2)}) async-start(), calls=%async_computation.4 | async-start | bytes 196608 | tf_op jit(solution)/shard_map/psum | solution.py:49
  7.2 5.8 copy-start.1
  14.5 2.7 copy-start.2
  26.9 23.8 %copy-start.4 = (s32[16]{0:T(128)S(1)}, s32[16]{0:T(128)}, u32[]{:S(2)}) copy-start(s32[16]{0:T(128)} %param.19) | copy-start | bytes 196
  50.9 26.9 %copy-start.5 = (s32[16]{0:T(128)}, s32[16]{0:T(128)S(1)}, u32[]{:S(2)}) copy-start(s32[16]{0:T(128)S(1)} %multiply_add_fusion.1) | copy-start | bytes 196
  51.8 13.9 %all-to-all-start.2 = ((s32[16,2,1]{1,2,0:T(1,128)}), s32[16,2,1]{1,2,0:T(1,128)}, u32[]{:S(2)}, u32[]{:S(2)}) async-start(s32[16,2,1]{1,2,0:T(1,128)} %bitcast.4), calls=%async_computation.2 | async-start | bytes 16384 | tf_op jit(solution)/shard_map/all_to_all | solution.py:74
  65.7 12.2 %all-to-all-start.3 = ((s32[16,2,1]{1,2,0:T(1,128)}), s32[16,2,1]{1,2,0:T(1,128)S(1)}, u32[]{:S(2)}, u32[]{:S(2)}) async-start(s32[16,2,1]{1,2,0:T(1,128)} %all-to-all-done.2), calls=%async_computation.3 | async-start | bytes 16384 | tf_op jit(solution)/shard_map/all_to_all | solution.py:73
  113.1 13.1 %all-to-all-start = ((bf16[16,2,192]{2,1,0:T(2,128)(2,1)}), bf16[16,2,192]{2,1,0:T(2,128)(2,1)}, u32[]{:S(2)}, u32[]{:S(2)}) async-start(bf16[16,2,192]{2,1,0:T(2,128)(2,1)} %reshape.84), calls=%async_computation | async-start | bytes 32768 | tf_op jit(solution)/shard_map/all_to_all | solution.py:67
  126.2 11.9 %all-to-all-start.1 = ((bf16[16,2,192]{2,1,0:T(2,128)(2,1)}), bf16[16,2,192]{2,1,0:T(2,128)(2,1)S(1)}, u32[]{:S(2)}, u32[]{:S(2)}) async-start(bf16[16,2,192]{2,1,0:T(2,128)(2,1)} %all-to-all-done), calls=%async_computation.1 | async-start | bytes 32768 | tf_op jit(solution)/shard_map/all_to_all | solution.py:66
  138.8 81.8 %all-reduce.8.cloned.1.call-start = ((), (), s32[]{:S(2)}) async-start(), calls=%async_computation.5 | async-start | bytes 393216 | tf_op jit(solution)/shard_map/while/body/eval_jaxpr/psum | solution.py:12
  220.6 5.8 copy-start.3
  358.2 83.2 %all-reduce.8.cloned.1.call-start = ((), (), s32[]{:S(2)}) async-start(), calls=%async_computation.5 | async-start | bytes 393216 | tf_op jit(solution)/shard_map/while/body/eval_jaxpr/psum | solution.py:12
  441.4 5.8 copy-start.3
  579.0 82.9 %all-reduce.8.cloned.1.call-start = ((), (), s32[]{:S(2)}) async-start(), calls=%async_computation.5 | async-start | bytes 393216 | tf_op jit(solution)/shard_map/while/body/eval_jaxpr/psum | solution.py:12
  661.9 5.8 copy-start.3
  799.5 82.9 %all-reduce.8.cloned.1.call-start = ((), (), s32[]{:S(2)}) async-start(), calls=%async_computation.5 | async-start | bytes 393216 | tf_op jit(solution)/shard_map/while/body/eval_jaxpr/psum | solution.py:12
  882.4 5.8 copy-start.3
Sparse Core Ops, SparseCore 0:
  50.9 59.5 all-reduce.5
  142.8 77.7 all-reduce.7
  362.2 79.1 all-reduce.7
  582.8 79.0 all-reduce.7
  803.2 79.1 all-reduce.7
where the time goes:
time: 1030 us
  blocking collectives  556 us (54%)
  waiting for transfers between devices  330 us (32%)
  matrix products  56.9 us (6%)
  starting transfers between devices  29 us (3%)
  other arithmetic  22 us (2%)
  local copies, waits for them, and re-layouts  15.6 us (2%)
  between operations  13.8 us (1%)
    psum x4, waiting for transfers between devices, spread(): return lax.psum(jnp.where(mine, x, jnp.zeros_like(x)), axis)  278 us
    pmax x4, blocking collectives, score_rows(): largest = lax.pmax(local_max, ('wide', 'narrow'))  265 us
    psum x4, blocking collectives, score_rows(): total, picked = lax.psum((local_total, local_positive), ('wide', 'narrow'))  250 us
    psum x4, blocking collectives, spread(): return lax.psum(jnp.where(mine, x, jnp.zeros_like(x)), axis)  40.4 us
    psum x1, waiting for transfers between devices, local(): pooled = lax.psum(pooled_part, 'narrow') + token_mean  32.4 us
    dot_general x4, matrix products, score_rows(): lax.dot_general(block, slab_old, contract, preferred_element_type=jnp.flo...  23.3 us
    dot_general x1, matrix products, local(): jnp.dot(hidden, down_weight, preferred_element_type=jnp.float32)  22.3 us
  transfers between devices with their start and end apart: 9, of which 9 were waited for; matrix products, arithmetic and copies ran while one was open for 0% of the time, Pallas kernels for 0%

commit v1 on v0

--- a/solution.py
+++ b/solution.py
@@ -9,7 +9,7 @@
 
 def spread(x, axis, root):
     mine = lax.axis_index(axis) == root
-    return lax.psum(jnp.where(mine, x, jnp.zeros_like(x)), axis)
+    return jnp.sum(lax.all_gather(jnp.where(mine, x, jnp.zeros_like(x)), axis), axis=0)
 
 
 def rms_scale(values):

time: 1030 us -> 894 us (0.87)
  waiting for transfers between devices: 330 us -> 168 us
  blocking collectives: 556 us -> 572 us
  other arithmetic: 22 us -> 34.4 us
    psum x4 -> x0, waiting for transfers between devices: 278 us -> none  [spread(): return lax.psum(jnp.where(mine, x, jnp.zeros_like(x)), axis)]
    all_gather x0 -> x4, waiting for transfers between devices: none -> 115 us  [spread(): lax.all_gather(jnp.where(mine, x, jnp.zeros_like(x)), axis)]
    all_gather x0 -> x4, blocking collectives: none -> 58.2 us  [spread(): lax.all_gather(jnp.where(mine, x, jnp.zeros_like(x)), axis)]
    psum x4 -> x0, blocking collectives: 40.4 us -> none  [spread(): return lax.psum(jnp.where(mine, x, jnp.zeros_like(x)), axis)]
    reduce_sum x0 -> x8, other arithmetic: none -> 12.4 us  [spread(): jnp.sum(lax.all_gather(jnp.where(mine, x, jnp.zeros_like(x)), axis), axis=0)]
where the time goes in v1:
time: 894 us; the launch traced here: 892 us
  blocking collectives  572 us (64%)
  waiting for transfers between devices  168 us (19%)
  matrix products  56.9 us (6%)
  other arithmetic  34.4 us (4%)
  starting transfers between devices  29 us (3%)
  local copies, waits for them, and re-layouts  15.6 us (2%)
  between operations  13.8 us (2%)
    pmax x4, blocking collectives, score_rows(): largest = lax.pmax(local_max, ('wide', 'narrow'))  259 us
    psum x4, blocking collectives, score_rows(): total, picked = lax.psum((local_total, local_positive), ('wide', 'narrow'))  254 us
    all_gather x4, waiting for transfers between devices, spread(): lax.all_gather(jnp.where(mine, x, jnp.zeros_like(x)), axis)  115 us
    all_gather x4, blocking collectives, spread(): lax.all_gather(jnp.where(mine, x, jnp.zeros_like(x)), axis)  58.2 us
    psum x1, waiting for transfers between devices, local(): pooled = lax.psum(pooled_part, 'narrow') + token_mean  32.4 us
    dot_general x4, matrix products, score_rows(): lax.dot_general(block, slab_old, contract, preferred_element_type=jnp.flo...  23.3 us
    dot_general x1, matrix products, local(): jnp.dot(hidden, down_weight, preferred_element_type=jnp.float32)  22.3 us
  transfers between devices with their start and end apart: 9, of which 9 were waited for; matrix products, arithmetic and copies ran while one was open for 0% of the time, Pallas kernels for 0%

profile of v1, /device:TPU:1, one launch (start us, length us, event | category | flops | bytes accessed | tf_op | source)
XLA Modules:
  0.0 892.1 jit_solution(16426637352766159025)
XLA Ops:
  17.2 9.7 %fusion.16 = f32[2048,1120]{0,1:T(8,128)} fusion(bf16[2048,1536]{1,0:T(8,128)(2,1)S(1)} %bitcast.46, bf16[1536,1120]{0,1:T(8,128)(2,1)S(1)} %copy-done), kind=kOutput, calls=%fused_computation.49 | convolution fusion | flops 7046430720 | bytes 18907136 | tf_op jit(solution)/shard_map/dot_general | solution.py:42
  26.9 22.3 %bitcast_reduce_fusion = f32[16,1536]{1,0:T(8,128)} fusion(bf16[1120,1536]{1,0:T(8,128)(2,1)} %param.17, bf16[2048,1536]{1,0:T(8,128)(2,1)} %bitcast.47, bf16[1536,1120]{0,1:T(8,128)(2,1)} %param.16, f32[2048,1120]{0,1:T(8,128)} %fusion.16), kind=kOutput, calls=%fused_computation.19 | convolution fusion | flops 14109745152 | bytes 22446080 | tf_op jit(solution)/shard_map/dot_general | solution.py:45
  51.8 7.6 all-to-all-start.2
  65.7 7.6 all-to-all-start.3
  78.1 32.4 %all-reduce.5.cloned.1.call-done = f32[16,1536]{1,0:T(8,128)} async-done(((f32[16,1536]{1,0:T(8,128)}), f32[16,1536]{1,0:T(8,128)}) %all-reduce.5.cloned.1.call-update) | async-done | bytes 98320 | tf_op jit(solution)/shard_map/psum | solution.py:49
  113.1 6.6 all-to-all-start
  126.2 7.2 all-to-all-start.1
  138.8 746.8 %while.16 = (s32[]{:T(128)}, f32[4,64]{1,0:T(4,128)}, s32[4]{0:T(128)}, bf16[1,64,1536]{2,1,0:T(8,128)(2,1)}, bf16[2048,1536]{1,0:T(8,128)(2,1)}, /*index=5*/pre...) while((s32[]{:T(128)}, f32[4,64]{1,0:T(4,128)}, ...), condition=%wide.region_19.20_spmd.clone, body=%wide.region_7.19_spmd.clone.sunk | while | flops 405935744 | bytes 22330420 | solution.py:122
  141.6 14.7 %all-gather.3 = s32[16,1,64]{2,1,0:T(1,128)S(1)} all-gather(s32[1,1,64]{2,1,0:T(1,128)S(1)} %fusion.37), channel_id=1, replica_groups=mesh['wide'=16,'narrow'=8] {'wide'}, dimensions={0}, use_global_device_ids=true | all-gather | bytes 4352 | tf_op jit(solution)/shard_map/while/body/eval_jaxpr/all_gather | solution.py:12
  156.4 28.1 %all-gather.6.cloned.1.call-done = bf16[16,64,1536]{2,1,0:T(8,128)(2,1)} async-done(((bf16[1,64,1536]{2,1,0:T(8,128)(2,1)}), bf16[16,64,1536]{2,1,0:T(8,128)(2,1)}) %all-gather.6.cloned.1.call-update) | async-done | bytes 3145744 | tf_op jit(solution)/shard_map/while/body/eval_jaxpr/all_gather | solution.py:12
  193.6 64.8 %pmax.16 = f32[64]{0:T(128)S(1)} all-reduce(f32[64]{0:T(128)S(1)} %max.14), channel_id=1, replica_groups=mesh['wide'=16,'narrow'=8] {'wide','narrow'}, use_global_device_ids=true, to_apply=%region_11.11 | all-reduce | flops 64 | bytes 512 | tf_op jit(solution)/shard_map/while/body/eval_jaxpr/pmax | solution.py:107
  259.9 63.5 %all-reduce.2 = (f32[64]{0:T(128)S(1)}, f32[64]{0:T(128)S(1)}) all-reduce(f32[64]{0:T(128)S(1)} %add.199, f32[64]{0:T(128)S(1)} %add.200), channel_id=1, replica_groups=mesh['wide'=16,'narrow'=8] {'wide','narrow'}, use_global_device_ids=true, to_apply=%region_18.18 | all-reduce | flops 128 | bytes 1024 | tf_op jit(solution)/shard_map/while/body/eval_jaxpr/psum | solution.py:112
  327.4 14.9 %all-gather.3 = s32[16,1,64]{2,1,0:T(1,128)S(1)} all-gather(s32[1,1,64]{2,1,0:T(1,128)S(1)} %fusion.37), channel_id=1, replica_groups=mesh['wide'=16,'narrow'=8] {'wide'}, dimensions={0}, use_global_device_ids=true | all-gather | bytes 4352 | tf_op jit(solution)/shard_map/while/body/eval_jaxpr/all_gather | solution.py:12
  342.4 29.4 %all-gather.6.cloned.1.call-done = bf16[16,64,1536]{2,1,0:T(8,128)(2,1)} async-done(((bf16[1,64,1536]{2,1,0:T(8,128)(2,1)}), bf16[16,64,1536]{2,1,0:T(8,128)(2,1)}) %all-gather.6.cloned.1.call-update) | async-done | bytes 3145744 | tf_op jit(solution)/shard_map/while/body/eval_jaxpr/all_gather | solution.py:12
  380.8 64.8 %pmax.16 = f32[64]{0:T(128)S(1)} all-reduce(f32[64]{0:T(128)S(1)} %max.14), channel_id=1, replica_groups=mesh['wide'=16,'narrow'=8] {'wide','narrow'}, use_global_device_ids=true, to_apply=%region_11.11 | all-reduce | flops 64 | bytes 512 | tf_op jit(solution)/shard_map/while/body/eval_jaxpr/pmax | solution.py:107
  447.1 63.5 %all-reduce.2 = (f32[64]{0:T(128)S(1)}, f32[64]{0:T(128)S(1)}) all-reduce(f32[64]{0:T(128)S(1)} %add.199, f32[64]{0:T(128)S(1)} %add.200), channel_id=1, replica_groups=mesh['wide'=16,'narrow'=8] {'wide','narrow'}, use_global_device_ids=true, to_apply=%region_18.18 | all-reduce | flops 128 | bytes 1024 | tf_op jit(solution)/shard_map/while/body/eval_jaxpr/psum | solution.py:112
  516.2 13.4 %all-gather.3 = s32[16,1,64]{2,1,0:T(1,128)S(1)} all-gather(s32[1,1,64]{2,1,0:T(1,128)S(1)} %fusion.37), channel_id=1, replica_groups=mesh['wide'=16,'narrow'=8] {'wide'}, dimensions={0}, use_global_device_ids=true | all-gather | bytes 4352 | tf_op jit(solution)/shard_map/while/body/eval_jaxpr/all_gather | solution.py:12
  529.7 28.5 %all-gather.6.cloned.1.call-done = bf16[16,64,1536]{2,1,0:T(8,128)(2,1)} async-done(((bf16[1,64,1536]{2,1,0:T(8,128)(2,1)}), bf16[16,64,1536]{2,1,0:T(8,128)(2,1)}) %all-gather.6.cloned.1.call-update) | async-done | bytes 3145744 | tf_op jit(solution)/shard_map/while/body/eval_jaxpr/all_gather | solution.py:12
  567.3 64.8 %pmax.16 = f32[64]{0:T(128)S(1)} all-reduce(f32[64]{0:T(128)S(1)} %max.14), channel_id=1, replica_groups=mesh['wide'=16,'narrow'=8] {'wide','narrow'}, use_global_device_ids=true, to_apply=%region_11.11 | all-reduce | flops 64 | bytes 512 | tf_op jit(solution)/shard_map/while/body/eval_jaxpr/pmax | solution.py:107
  633.6 63.5 %all-reduce.2 = (f32[64]{0:T(128)S(1)}, f32[64]{0:T(128)S(1)}) all-reduce(f32[64]{0:T(128)S(1)} %add.199, f32[64]{0:T(128)S(1)} %add.200), channel_id=1, replica_groups=mesh['wide'=16,'narrow'=8] {'wide','narrow'}, use_global_device_ids=true, to_apply=%region_18.18 | all-reduce | flops 128 | bytes 1024 | tf_op jit(solution)/shard_map/while/body/eval_jaxpr/psum | solution.py:112
  701.1 15.2 %all-gather.3 = s32[16,1,64]{2,1,0:T(1,128)S(1)} all-gather(s32[1,1,64]{2,1,0:T(1,128)S(1)} %fusion.37), channel_id=1, replica_groups=mesh['wide'=16,'narrow'=8] {'wide'}, dimensions={0}, use_global_device_ids=true | all-gather | bytes 4352 | tf_op jit(solution)/shard_map/while/body/eval_jaxpr/all_gather | solution.py:12
  716.4 29.0 %all-gather.6.cloned.1.call-done = bf16[16,64,1536]{2,1,0:T(8,128)(2,1)} async-done(((bf16[1,64,1536]{2,1,0:T(8,128)(2,1)}), bf16[16,64,1536]{2,1,0:T(8,128)(2,1)}) %all-gather.6.cloned.1.call-update) | async-done | bytes 3145744 | tf_op jit(solution)/shard_map/while/body/eval_jaxpr/all_gather | solution.py:12
  754.5 64.8 %pmax.16 = f32[64]{0:T(128)S(1)} all-reduce(f32[64]{0:T(128)S(1)} %max.14), channel_id=1, replica_groups=mesh['wide'=16,'narrow'=8] {'wide','narrow'}, use_global_device_ids=true, to_apply=%region_11.11 | all-reduce | flops 64 | bytes 512 | tf_op jit(solution)/shard_map/while/body/eval_jaxpr/pmax | solution.py:107
  820.8 63.5 %all-reduce.2 = (f32[64]{0:T(128)S(1)}, f32[64]{0:T(128)S(1)}) all-reduce(f32[64]{0:T(128)S(1)} %add.199, f32[64]{0:T(128)S(1)} %add.200), channel_id=1, replica_groups=mesh['wide'=16,'narrow'=8] {'wide','narrow'}, use_global_device_ids=true, to_apply=%region_18.18 | all-reduce | flops 128 | bytes 1024 | tf_op jit(solution)/shard_map/while/body/eval_jaxpr/psum | solution.py:112
  (118 shorter events, 95.3 us)
Async XLA Ops:
  7.2 10.1 %copy-start = (bf16[1536,1120]{0,1:T(8,128)(2,1)S(1)}, bf16[1536,1120]{0,1:T(8,128)(2,1)}, u32[]{:S(2)}) copy-start(bf16[1536,1120]{0,1:T(8,128)(2,1)} %param.15) | copy-start | bytes 10321924
  7.2 103.3 %all-reduce.5.cloned.1.call-start = ((), (), s32[]{:S(2)}) async-start(), calls=%async_computation.4 | async-start | bytes 196608 | tf_op jit(solution)/shard_map/psum | solution.py:49
  7.2 5.8 copy-start.1
  14.5 2.7 copy-start.3
  26.9 23.8 %copy-start.4 = (s32[16]{0:T(128)S(1)}, s32[16]{0:T(128)}, u32[]{:S(2)}) copy-start(s32[16]{0:T(128)} %param.19) | copy-start | bytes 196
  50.9 26.9 %copy-start.5 = (s32[16]{0:T(128)}, s32[16]{0:T(128)S(1)}, u32[]{:S(2)}) copy-start(s32[16]{0:T(128)S(1)} %multiply_add_fusion.1) | copy-start | bytes 196
  51.8 13.9 %all-to-all-start.2 = ((s32[16,2,1]{1,2,0:T(1,128)}), s32[16,2,1]{1,2,0:T(1,128)}, u32[]{:S(2)}, u32[]{:S(2)}) async-start(s32[16,2,1]{1,2,0:T(1,128)} %bitcast.4), calls=%async_computation.2 | async-start | bytes 16384 | tf_op jit(solution)/shard_map/all_to_all | solution.py:74
  65.7 12.2 %all-to-all-start.3 = ((s32[16,2,1]{1,2,0:T(1,128)}), s32[16,2,1]{1,2,0:T(1,128)S(1)}, u32[]{:S(2)}, u32[]{:S(2)}) async-start(s32[16,2,1]{1,2,0:T(1,128)} %all-to-all-done.2), calls=%async_computation.3 | async-start | bytes 16384 | tf_op jit(solution)/shard_map/all_to_all | solution.py:73
  113.1 13.1 %all-to-all-start = ((bf16[16,2,192]{2,1,0:T(2,128)(2,1)}), bf16[16,2,192]{2,1,0:T(2,128)(2,1)}, u32[]{:S(2)}, u32[]{:S(2)}) async-start(bf16[16,2,192]{2,1,0:T(2,128)(2,1)} %reshape.90), calls=%async_computation | async-start | bytes 32768 | tf_op jit(solution)/shard_map/all_to_all | solution.py:67
  126.2 11.9 %all-to-all-start.1 = ((bf16[16,2,192]{2,1,0:T(2,128)(2,1)}), bf16[16,2,192]{2,1,0:T(2,128)(2,1)S(1)}, u32[]{:S(2)}, u32[]{:S(2)}) async-start(bf16[16,2,192]{2,1,0:T(2,128)(2,1)} %all-to-all-done), calls=%async_computation.1 | async-start | bytes 32768 | tf_op jit(solution)/shard_map/all_to_all | solution.py:66
  138.8 45.7 %all-gather.6.cloned.1.call-start = ((), (), s32[]{:S(2)}) async-start(), calls=%async_computation.5 | async-start | bytes 3342336 | tf_op jit(solution)/shard_map/while/body/eval_jaxpr/all_gather | solution.py:12
  187.6 5.8 copy-start.2
  324.7 47.0 %all-gather.6.cloned.1.call-start = ((), (), s32[]{:S(2)}) async-start(), calls=%async_computation.5 | async-start | bytes 3342336 | tf_op jit(solution)/shard_map/while/body/eval_jaxpr/all_gather | solution.py:12
  374.8 5.8 copy-start.2
  511.9 46.3 %all-gather.6.cloned.1.call-start = ((), (), s32[]{:S(2)}) async-start(), calls=%async_computation.5 | async-start | bytes 3342336 | tf_op jit(solution)/shard_map/while/body/eval_jaxpr/all_gather | solution.py:12
  561.3 5.8 copy-start.2
  698.4 47.0 %all-gather.6.cloned.1.call-start = ((), (), s32[]{:S(2)}) async-start(), calls=%async_computation.5 | async-start | bytes 3342336 | tf_op jit(solution)/shard_map/while/body/eval_jaxpr/all_gather | solution.py:12
  748.5 5.8 copy-start.2
Sparse Core Ops, SparseCore 0:
  50.9 59.5 all-reduce.4
  141.8 42.7 all-gather.5
  327.6 44.0 all-gather.5
  515.7 42.5 all-gather.5
  701.2 44.1 all-gather.5
